TPU v7x, 512 devices: a whole 4x4x16 slice. The times are simulated.
512 devices in a mesh: tile: 32 (over z_lo, y, core), date: 16 (over z_hi, x).
Axes of the slice: x: 4, y: 4, z: 16 (z_hi: 4, z_lo: 4; z = z_hi * 4 + z_lo), core: 2. Of those that a mesh axis runs over, the one named last changes fastest.
Arguments:
- secondary: bfloat16 [16, 2, 3072, 1024], P('date', None, 'tile'), may hold values from -6 to 6
- primary: bfloat16 [2, 3072, 1024], P(None, 'tile', 'date'), may hold values from -6 to 6
- margin_mask: int32 [3072], P('tile'), may hold values from 0 to 1, as said below
- az_off: int32 [16, 32], P('date', 'tile'), may hold values from -16 to 16
- rg_off: int32 [16, 32], P('date', 'tile'), may hold values from -16 to 16
- az_frac: float32 [16, 32], P('date', 'tile'), may hold values from 0 to 1
- rg_frac: float32 [16, 32], P('date', 'tile'), may hold values from 0 to 1
Outputs:
- looks: float32 [16, 2, 1536, 128], P('date', None, 'tile')
Inputs may be any that keep to these rules, and one draw needn't show every extreme that they name: `margin_mask`: ones lie only in the last 64 rows of each tile of 96 rows, and the last row of every tile is 1.
All inputs are finite; a program needn't handle non-finite values.
Results may differ from a plain program's by a relative error of at most 0.017.
Values may be sent and summed in bfloat16 or wider, within the bound.
A program may use at most 64 MiB of HBM per device.

v0:
```python
import jax
import jax.numpy as jnp
from jax import lax
from jax.sharding import PartitionSpec as P

KA = 16
LAG = 64
LA = 2
LR = 8


def padded(block, sides, width):
    for axis, dim in sides:
        count = lax.axis_size(axis)
        forward = [(i, i + 1) for i in range(count - 1)]
        backward = [(target, source) for source, target in forward]
        low = lax.ppermute(
            lax.slice_in_dim(block, block.shape[dim] - width, None, axis=dim), axis, forward
        )
        high = lax.ppermute(lax.slice_in_dim(block, 0, width, axis=dim), axis, backward)
        block = jnp.concatenate([low, block, high], axis=dim)
    return block


def passed_along(value, axis, steps):
    count = lax.axis_size(axis)
    initial, last = (max(0, -steps), min(count, count - steps))
    return lax.ppermute(value, axis, [(source, source + steps) for source in range(initial, last)])


def window(dist):
    return jnp.sinc(dist) * (0.5 + 0.5 * jnp.cos(jnp.pi * dist / 4.0))


def band_taps(offset, frac):
    inside = (offset >= -3) & (offset <= 4)
    return jnp.where(inside, window(offset.astype(jnp.float32) - frac), 0.0).astype(jnp.bfloat16)


def multilook(values):
    depth, rows_n, cols_n = values.shape
    return values.reshape(depth, rows_n // LA, LA, cols_n // LR, LR).mean(axis=(2, 4))


def shards(secondary, primary, margin_mask, az_off, rg_off, az_frac, rg_frac):
    rim_rows = KA + 4
    block_cols = 256
    image = secondary[0]
    rows_n = image.shape[1]
    cols_n = image.shape[2]
    extended = padded(image, (("tile", 1),), rim_rows)
    row_out = lax.broadcasted_iota(jnp.int32, (rows_n, rows_n + 2 * rim_rows), 0)
    row_in = lax.broadcasted_iota(jnp.int32, (rows_n, rows_n + 2 * rim_rows), 1)
    azim_taps = band_taps(row_in - row_out - az_off[0, 0] - rim_rows, az_frac[0, 0])
    azim = jnp.einsum(
        "im,kmc->kic", azim_taps, extended, preferred_element_type=jnp.float32
    ).astype(jnp.bfloat16)
    blocks_n = cols_n // block_cols
    col_pad = jnp.pad(azim, ((0, 0), (0, 0), (block_cols // 2, block_cols // 2)))
    pieces = col_pad.reshape(2, rows_n, blocks_n + 1, block_cols)
    inputs = jnp.concatenate([pieces[:, :, :-1], pieces[:, :, 1:]], axis=3)
    col_in = lax.broadcasted_iota(jnp.int32, (2 * block_cols, block_cols), 0)
    col_out = lax.broadcasted_iota(jnp.int32, (2 * block_cols, block_cols), 1)
    range_taps = band_taps(col_in - block_cols // 2 - col_out - rg_off[0, 0], rg_frac[0, 0])
    resampled = jnp.einsum("kibm,mn->kibn", inputs, range_taps, preferred_element_type=jnp.float32)
    resampled = resampled.reshape(2, rows_n, cols_n).astype(jnp.bfloat16)
    prim = lax.all_gather(primary, "date", axis=2, tiled=True)[None]
    moved = resampled[None]
    sec_f = moved.astype(jnp.float32)
    prim_f = prim.astype(jnp.float32)
    ifg_re = prim_f[:, 0] * sec_f[:, 0] + prim_f[:, 1] * sec_f[:, 1]
    ifg_im = prim_f[:, 1] * sec_f[:, 0] - prim_f[:, 0] * sec_f[:, 1]
    interf = jnp.stack((ifg_re, ifg_im), axis=1)
    upcoming = passed_along(interf[:, :, :LAG, :], "tile", -1)
    later = jnp.concatenate([interf[:, :, LAG:, :], upcoming], axis=2)
    l_re = later[:, 0]
    l_im = later[:, 1]
    weight = margin_mask.astype(jnp.float32)[None, :, None]
    e_re = jnp.sum(weight * (ifg_re * l_re + ifg_im * l_im), axis=(1, 2))
    e_im = jnp.sum(weight * (ifg_im * l_re - ifg_re * l_im), axis=(1, 2))
    power = jnp.sum(
        weight * 0.5 * (ifg_re * ifg_re + ifg_im * ifg_im + l_re * l_re + l_im * l_im), axis=(1, 2)
    )
    count = jnp.zeros_like(e_re) + jnp.sum(margin_mask.astype(jnp.float32)) * interf.shape[3]
    stats = jnp.stack((e_re, e_im, power, count), axis=1)
    totals = lax.psum(stats, "tile")
    magnitude = jnp.sqrt(totals[:, 0] * totals[:, 0] + totals[:, 1] * totals[:, 1])
    floor_val = (totals[:, 2] + 1e-06) / jnp.sqrt(jnp.maximum(totals[:, 3], 1.0))
    denom = jnp.maximum(magnitude, floor_val)
    u_re = (totals[:, 0] / denom)[:, None, None]
    u_im = (totals[:, 1] / denom)[:, None, None]
    c_re = multilook(ifg_re * u_re + ifg_im * u_im)
    c_im = multilook(ifg_im * u_re - ifg_re * u_im)
    result = jnp.stack((c_re, c_im), axis=1)
    return result


def solution(mesh):
    return jax.shard_map(
        shards,
        mesh=mesh,
        in_specs=(
            P("date", None, "tile", None),
            P(None, "tile", "date"),
            P("tile"),
            P("date", "tile"),
            P("date", "tile"),
            P("date", "tile"),
            P("date", "tile"),
        ),
        out_specs=P("date", None, "tile", None),
        check_vma=False,
    )
```

profile of v0, /device:TPU:1, one launch (start us, length us, event | category | flops | bytes accessed | tf_op | source)
XLA Modules:
  0.0 181.6 jit_solution(2312911935924852726)
XLA Ops:
  0.0 0.0 copy-start
  0.0 1.0 fusion.116
  1.0 4.6 %collective-permute-start = (bf16[2,20,1024]{2,1,0:T(8,128)(2,1)S(1)}, bf16[2,20,1024]{2,1,0:T(8,128)(2,1)S(1)}, u32[]{:S(2)}, u32[]{:S(2)}) collective-permute-start(bf16[2,20,1024]{2,1,0:T(8,128)(2,1)S(1)} %get-tuple-element.14), channel_id=1, source_target_pairs={{0,16},{16,32},{32,48},{48,64},{64,80},{80,96},{96,112},{112,128},... | collective-permute-start | bytes 245768 | tf_op jit(solution)/shard_map/ppermute | solution.py:17
  5.6 5.5 %collective-permute-start.1 = (bf16[2,20,1024]{2,1,0:T(8,128)(2,1)S(1)}, bf16[2,20,1024]{2,1,0:T(8,128)(2,1)S(1)}, u32[]{:S(2)}, u32[]{:S(2)}) collective-permute-start(bf16[2,20,1024]{2,1,0:T(8,128)(2,1)S(1)} %get-tuple-element.15), channel_id=1, source_target_pairs={{16,0},{32,16},{48,32},{64,48},{80,64},{96,80},{112,96},{128,112},... | collective-permute-start | bytes 245768 | tf_op jit(solution)/shard_map/ppermute | solution.py:20
  13.7 0.8 copy.15
  14.5 55.4 %all_gather.3 = bf16[2,96,1024]{1,0,2:T(2,128)(2,1)S(1)} all-gather(bf16[2,96,64]{1,0,2:T(2,128)(2,1)S(1)} %copy.15), channel_id=1, replica_groups=mesh['tile'=32,'date'=16] {'date'}, dimensions={2}, use_global_device_ids=true | all-gather | bytes 417792 | tf_op jit(solution)/shard_map/all_gather | solution.py:67
  69.9 0.4 copy.16
  70.3 0.1 bitcast_convert_fusion
  70.4 0.0 collective-permute-done
  70.4 0.0 collective-permute-done.1
  70.4 0.0 copy-done
  70.4 0.6 fusion.1
  71.1 0.3 copy.24
  71.3 0.1 pad.4.clone
  71.5 0.2 fusion.115
  71.7 0.2 copy.22
  71.9 0.2 copy.23
  72.1 2.9 %fusion = f32[2,96,4,256]{3,1,2,0:T(8,128)S(1)} fusion(bf16[2,96,4,256]{3,1,2,0:T(8,128)(2,1)S(1)} %copy.23, bf16[2,96,4,256]{3,1,2,0:T(8,128)(2,1)S(1)} %copy.22, f32[]{:T(128)} %bitcast.51, s32[]{:T(128)} %bitcast.49, s32[512]{0:T(512)S(1)} %iota_add_fusion), kind=kOutput, calls=%fused_computation.2 | convolution fusion | flops 209321984 | bytes 1574920 | tf_op jit(solution)/shard_map/kibm,mn->kibn/dot_general | solution.py:65
  75.0 0.5 copy.20
  75.5 0.4 reshape.581
  75.9 0.0 copy-start.1
  75.9 0.2 multiply_subtract_fusion.1
  76.1 3.9 %collective-permute-start.2 = (f32[1,2,64,1024]{3,2,1,0:T(8,128)S(1)}, f32[1,2,64,1024]{3,2,1,0:T(8,128)S(1)}, u32[]{:S(2)}, u32[]{:S(2)}) collective-permute-start(f32[1,2,64,1024]{3,2,1,0:T(8,128)S(1)} %pad_maximum_fusion.1), channel_id=1, source_target_pairs={{16,0},{32,16},{48,32},{64,48},{80,64},{96,80},{112,96},{128,112},... | collective-permute-start | bytes 1572872 | tf_op jit(solution)/shard_map/ppermute | solution.py:28
  80.0 0.0 copy-done.1
  80.0 0.6 broadcast_multiply_fusion
  81.3 12.3 %collective-permute-done.2 = f32[1,2,64,1024]{3,2,1,0:T(8,128)S(1)} collective-permute-done((f32[1,2,64,1024]{3,2,1,0:T(8,128)S(1)}, f32[1,2,64,1024]{3,2,1,0:T(8,128)S(1)}, u32[]{:S(2)}, u32[]{:S(2)}) %collective-permute-start.2) | collective-permute-done | bytes 524320 | tf_op jit(solution)/shard_map/ppermute | solution.py:28
  93.6 0.1 fusion.2
  93.7 1.0 fusion.29
  94.7 2.0 %pad_maximum_fusion.3 = f32[1,4]{1,0:T(1,128)S(1)} fusion(f32[1,1]{1,0:T(1,128)} %bitcast.18, f32[1,1]{1,0:T(1,128)} %bitcast.17, f32[1,1]{1,0:T(1,128)} %bitcast.15, f32[1,1]{1,0:T(1,128)} %bitcast.13), kind=kLoop, calls=%fused_computation.124 | loop fusion | flops 12 | bytes 32 | tf_op jit(solution)/shard_map/stack | solution.py:85
  96.6 61.0 %psum.7 = f32[1,4]{1,0:T(1,128)S(1)} all-reduce(f32[1,4]{1,0:T(1,128)S(1)} %pad_maximum_fusion.3), channel_id=1, replica_groups=mesh['tile'=32,'date'=16] {'tile'}, use_global_device_ids=true, to_apply=%region_4.5 | all-reduce | flops 4 | bytes 32 | tf_op jit(solution)/shard_map/psum | solution.py:86
  157.7 0.6 fusion.117
  163.6 0.1 multiply_add_fusion.1
  163.7 5.0 %add.275 = f32[48,2,128,8]{3,2,1,0:T(8,128)} reshape(f32[1,1,96,1024]{3,2,1,0:T(8,128)S(1)} %get-tuple-element.10) | data formatting | bytes 786432 | tf_op jit(solution)/shard_map/add | solution.py:92
  168.6 5.0 %sub.152 = f32[48,2,128,8]{3,2,1,0:T(8,128)} reshape(f32[1,1,96,1024]{3,2,1,0:T(8,128)S(1)} %get-tuple-element.11) | data formatting | bytes 786432 | tf_op jit(solution)/shard_map/sub | solution.py:93
  173.6 3.7 %reduce_sum.58 = f32[48,128]{1,0:T(8,128)S(1)} reduce(f32[48,2,128,8]{3,2,1,0:T(8,128)} %add.275, f32[]{:T(128)} %constant.55.clone.1), dimensions={1,3}, to_apply=%region_5.6 | reduce | flops 92160 | bytes 417796 | tf_op jit(solution)/shard_map/reduce_sum | solution.py:42
  177.3 3.7 %reduce_sum.59 = f32[48,128]{1,0:T(8,128)S(1)} reduce(f32[48,2,128,8]{3,2,1,0:T(8,128)} %sub.152, f32[]{:T(128)} %constant.55.clone.1), dimensions={1,3}, to_apply=%region_6.7 | reduce | flops 92160 | bytes 417796 | tf_op jit(solution)/shard_map/reduce_sum | solution.py:42
  181.0 0.6 pad_maximum_fusion.2
  (4 shorter events, 0.1 us)
Async XLA Ops:
  0.0 70.4 %copy-start = (bf16[1,2,96,1024]{3,2,1,0:T(8,128)(2,1)S(1)}, bf16[1,2,96,1024]{3,2,1,0:T(8,128)(2,1)}, u32[]{:S(2)}) copy-start(bf16[1,2,96,1024]{3,2,1,0:T(8,128)(2,1)} %param.7) | copy-start | bytes 1179652
  1.0 69.4 %collective-permute-start = (bf16[2,20,1024]{2,1,0:T(8,128)(2,1)S(1)}, bf16[2,20,1024]{2,1,0:T(8,128)(2,1)S(1)}, u32[]{:S(2)}, u32[]{:S(2)}) collective-permute-start(bf16[2,20,1024]{2,1,0:T(8,128)(2,1)S(1)} %get-tuple-element.14), channel_id=1, source_target_pairs={{0,16},{16,32},{32,48},{48,64},{64,80},{80,96},{96,112},{112,128},... | collective-permute-start | bytes 245768 | tf_op jit(solution)/shard_map/ppermute | solution.py:17
  5.6 64.8 %collective-permute-start.1 = (bf16[2,20,1024]{2,1,0:T(8,128)(2,1)S(1)}, bf16[2,20,1024]{2,1,0:T(8,128)(2,1)S(1)}, u32[]{:S(2)}, u32[]{:S(2)}) collective-permute-start(bf16[2,20,1024]{2,1,0:T(8,128)(2,1)S(1)} %get-tuple-element.15), channel_id=1, source_target_pairs={{16,0},{32,16},{48,32},{64,48},{80,64},{96,80},{112,96},{128,112},... | collective-permute-start | bytes 245768 | tf_op jit(solution)/shard_map/ppermute | solution.py:20
  75.9 4.1 %copy-start.1 = (s32[96]{0:T(128)S(1)}, s32[96]{0:T(128)}, u32[]{:S(2)}) copy-start(s32[96]{0:T(128)} %param.9) | copy-start | bytes 1156
  76.1 17.5 %collective-permute-start.2 = (f32[1,2,64,1024]{3,2,1,0:T(8,128)S(1)}, f32[1,2,64,1024]{3,2,1,0:T(8,128)S(1)}, u32[]{:S(2)}, u32[]{:S(2)}) collective-permute-start(f32[1,2,64,1024]{3,2,1,0:T(8,128)S(1)} %pad_maximum_fusion.1), channel_id=1, source_target_pairs={{16,0},{32,16},{48,32},{64,48},{80,64},{96,80},{112,96},{128,112},... | collective-permute-start | bytes 1572872 | tf_op jit(solution)/shard_map/ppermute | solution.py:28
where the time goes:
time: 182 us
  blocking collectives  116 us (64%)
  local copies, waits for them, and re-layouts  14.7 us (8%)
  starting transfers between devices  13.9 us (8%)
  waiting for transfers between devices  12.3 us (7%)
  other arithmetic  12 us (7%)
  between operations  8.73 us (5%)
  matrix products  3.52 us (2%)
    psum x1, blocking collectives, shards(): totals = lax.psum(stats, 'tile')  61 us
    all_gather x1, blocking collectives, shards(): prim = lax.all_gather(primary, 'date', axis=2, tiled=True)[None]  55.4 us
    ppermute x1, waiting for transfers between devices, passed_along(): lax.ppermute(value, axis, [(source, source + steps) for source in range(i...  12.3 us
    reduce_sum x2, other arithmetic, multilook(): values.reshape(depth, rows_n // LA, LA, cols_n // LR, LR).mean(axis=(2, 4))  7.34 us
    ppermute x1, starting transfers between devices, padded(): lax.ppermute(lax.slice_in_dim(block, 0, width, axis=dim), axis, backward)  5.46 us
    sub x1, local copies, waits for them, and re-layouts, shards(): c_im = multilook(ifg_im * u_re - ifg_re * u_im)  4.97 us
    add x1, local copies, waits for them, and re-layouts, shards(): c_re = multilook(ifg_re * u_re + ifg_im * u_im)  4.95 us
    ppermute x1, starting transfers between devices, padded(): lax.ppermute(lax.slice_in_dim(block, block.shape[dim] - width, None, axis...  4.58 us
  transfers between devices with their start and end apart: 3, of which 1 were waited for; matrix products, arithmetic and copies ran while one was open for 1% of the time, Pallas kernels for 0%

commit v1 on v0

v1 whole, which is shorter than its diff:
```python
import functools

import jax
import jax.numpy as jnp
from jax import lax
from jax.experimental import pallas as pl
from jax.experimental.pallas import tpu as pltpu
from jax.sharding import PartitionSpec as P

LAG = 64
LA = 2
LR = 8
NX = 4
RIM = 32
SIDE = 128
BLOCK = 256
MESH = pl.DeviceIdType.MESH
F32 = jnp.float32
BF16 = jnp.bfloat16


def iota(shape, dim):
    return lax.broadcasted_iota(jnp.int32, shape, dim)


def tap_rows(frac, lanes):
    dist = iota((8, lanes), 0).astype(F32) - 3.0 - frac
    arg = jnp.pi * dist
    sinc = jnp.where(dist == 0.0, 1.0, jnp.sin(arg) / jnp.where(dist == 0.0, 1.0, arg))
    return sinc * (0.5 + 0.5 * jnp.cos(arg * 0.25))


def band(rows, first):
    total = jnp.zeros(first.shape, F32)
    for j in range(8):
        total = jnp.where(first == j - 3, rows[j : j + 1], total)
    return total.astype(BF16)


def kernel(
    tiles, dates,
    sec, prim, mask, az_off, rg_off, az_frac, rg_frac,
    out,
    ext, prim_in, azim, gath, res, ifg, lag_out, lag_in, stat_out, stat_in, acc,
    local_sem, halo_send, halo_recv, z_send, z_recv, x_send, x_recv,
    lag_send, lag_recv, stat_send, stat_recv,
):
    nz = dates // NX
    rows_n = sec.shape[2]
    cols_n = sec.shape[3]
    width = prim.shape[2]
    chunks = cols_n // 128
    t = lax.axis_index("tile")
    d = lax.axis_index("date")
    zh, x = d // NX, lax.rem(d, NX)
    step = 1 - 2 * lax.rem(t, 2)

    def z_at(k):
        return lax.rem(zh + k * step + 2 * nz, nz)

    def date_at(z, xx):
        return z * NX + xx

    def remote(src, dst, ss, rs, tile, date):
        return pltpu.make_async_remote_copy(
            src_ref=src, dst_ref=dst, send_sem=ss, recv_sem=rs,
            device_id={"tile": tile, "date": date}, device_id_type=MESH,
        )

    barrier = pltpu.get_barrier_semaphore()
    partners = 0
    for k in range(1, NX):
        pl.semaphore_signal(barrier, inc=1, device_id={"tile": t, "date": date_at(zh, lax.rem(x + k, NX))}, device_id_type=MESH)
        partners += 1
    for k in (1, -1):
        pl.semaphore_signal(barrier, inc=1, device_id={"tile": t, "date": date_at(z_at(k), x)}, device_id_type=MESH)
        partners += 1
    for k in range(1, tiles):
        pl.semaphore_signal(barrier, inc=1, device_id={"tile": lax.rem(t + k, tiles), "date": d}, device_id_type=MESH)
        partners += 1

    prim_copy = pltpu.make_async_copy(prim, prim_in, local_sem.at[0])
    prim_copy.start()
    own_copy = pltpu.make_async_copy(sec.at[0], ext.at[:, pl.ds(RIM, rows_n), :], local_sem.at[1])
    own_copy.start()

    @pl.when(t == 0)
    def _():
        ext[:, pl.ds(0, RIM), :] = jnp.zeros((2, RIM, cols_n), BF16)

    @pl.when(t == tiles - 1)
    def _():
        ext[:, pl.ds(RIM + rows_n, RIM), :] = jnp.zeros((2, RIM, cols_n), BF16)
        lag_in[...] = jnp.zeros(lag_in.shape, BF16)

    prim_copy.wait()
    mine = gath.at[zh, x]
    mine[:, pl.ds(0, width)] = prim_in[0]
    mine[:, pl.ds(width, width)] = prim_in[1]

    az_rows = tap_rows(az_frac[0, 0], 256)
    rg_rows = tap_rows(rg_frac[0, 0], 256)
    span = rows_n + 2 * RIM
    az_taps = band(az_rows[:, :span], iota((rows_n, span), 1) - iota((rows_n, span), 0) - (az_off[0, 0] + RIM))
    rg_shape = (BLOCK + 2 * SIDE, BLOCK)
    rg_taps = band(rg_rows, iota(rg_shape, 0) - iota(rg_shape, 1) - (rg_off[0, 0] + SIDE))
    azim[:, pl.ds(0, SIDE)] = jnp.zeros((2 * rows_n, SIDE), BF16)
    azim[:, pl.ds(SIDE + cols_n, SIDE)] = jnp.zeros((2 * rows_n, SIDE), BF16)
    lanes = iota((1, mask.shape[1]), 1)
    marks = jnp.where(mask[...] != 0, 1.0, 0.0).astype(F32)
    picked = iota((LAG, mask.shape[1]), 1) == iota((LAG, mask.shape[1]), 0) + (rows_n - LAG)
    weight = jnp.sum(jnp.where(picked, marks, 0.0), axis=1, keepdims=True)
    count = jnp.sum(marks, axis=1, keepdims=True) * float(cols_n)

    pl.semaphore_wait(barrier, partners)

    z_copies = [
        remote(mine, mine, z_send.at[0], z_recv.at[0], t, date_at(z_at(1), x)),
        remote(mine, mine, z_send.at[1], z_recv.at[1], t, date_at(z_at(-1), x)),
    ]
    z_copies[0].start()
    z_copies[1].start()

    def spread(group, z):
        block = gath.at[z, x]
        copies = [
            remote(block, block, x_send.at[group, k - 1], x_recv.at[group, k - 1], t, date_at(zh, lax.rem(x + k, NX)))
            for k in (2, 1, 3)
        ]
        for copy in copies:
            copy.start()
        return copies

    x_copies = {0: spread(0, zh)}

    up = remote(sec.at[0, :, pl.ds(rows_n - RIM, RIM), :], ext.at[:, pl.ds(0, RIM), :], halo_send.at[0], halo_recv.at[0], lax.rem(t + 1, tiles), d)
    down = remote(sec.at[0, :, pl.ds(0, RIM), :], ext.at[:, pl.ds(RIM + rows_n, RIM), :], halo_send.at[1], halo_recv.at[1], lax.rem(t + tiles - 1, tiles), d)

    @pl.when(t < tiles - 1)
    def _():
        up.start()

    @pl.when(t > 0)
    def _():
        down.start()

    own_copy.wait()

    @pl.when(t > 0)
    def _():
        up.wait_recv()

    @pl.when(t < tiles - 1)
    def _():
        down.wait_recv()

    for plane in range(2):
        for b in range(cols_n // BLOCK):
            part = jnp.dot(az_taps, ext[plane, :, pl.ds(b * BLOCK, BLOCK)], preferred_element_type=F32)
            azim[pl.ds(plane * rows_n, rows_n), pl.ds(SIDE + b * BLOCK, BLOCK)] = part.astype(BF16)

    near = gath.at[z_at(-1), x]
    z_copies[0].wait_recv()
    relay = remote(near, near, z_send.at[2], z_recv.at[2], t, date_at(z_at(1), x))
    relay.start()
    x_copies[1] = spread(1, z_at(-1))
    z_copies[1].wait_recv()
    x_copies[2] = spread(2, z_at(1))

    for b in range(cols_n // BLOCK):
        part = jnp.dot(azim[:, pl.ds(b * BLOCK, BLOCK + 2 * SIDE)], rg_taps, preferred_element_type=F32).astype(BF16)
        for h in range(BLOCK // 128):
            half = part[:, h * 128 : (h + 1) * 128]
            res[b * (BLOCK // 128) + h] = half

    low_half = iota((rows_n, 128), 1) < width

    def beat(group, z):
        for copy in x_copies[group]:
            copy.wait_recv()
        for q in range(NX // 2):
            m = z * (NX // 2) + q
            a = gath[z, 2 * q].astype(F32)
            b = gath[z, 2 * q + 1].astype(F32)
            p_re = jnp.where(low_half, a, pltpu.roll(b, width, 1))
            p_im = jnp.where(low_half, pltpu.roll(a, width, 1), b)
            r_re = res[m, pl.ds(0, rows_n)].astype(F32)
            r_im = res[m, pl.ds(rows_n, rows_n)].astype(F32)
            i_re = p_re * r_re + p_im * r_im
            i_im = p_im * r_re - p_re * r_im
            ifg[m, pl.ds(0, rows_n)] = i_re
            ifg[m, pl.ds(rows_n, rows_n)] = i_im
            lag_out[z, q, 0] = i_re[:LAG].astype(BF16)
            lag_out[z, q, 1] = i_im[:LAG].astype(BF16)

    def lag_copy(z):
        return remote(lag_out.at[z], lag_in.at[z], lag_send.at[z], lag_recv.at[z], lax.rem(t + tiles - 1, tiles), d)

    def send_lag(z):
        @pl.when(t > 0)
        def _():
            lag_copy(z).start()

    zeros = jnp.zeros((8, 128), F32)

    def fold(v):
        return jnp.sum(v.reshape(LAG // 8, 8, 128), axis=0)

    def margin(z, sums):
        @pl.when(t < tiles - 1)
        def _():
            lag_copy(z).wait_recv()

        e_re, e_im, power = sums
        for q in range(NX // 2):
            m = z * (NX // 2) + q
            a_re = ifg[m, pl.ds(rows_n - LAG, LAG)]
            a_im = ifg[m, pl.ds(2 * rows_n - LAG, LAG)]
            l_re = lag_in[z, q, 0].astype(F32)
            l_im = lag_in[z, q, 1].astype(F32)
            e_re += fold(weight * (a_re * l_re + a_im * l_im))
            e_im += fold(weight * (a_im * l_re - a_re * l_im))
            power += fold((0.5 * weight) * (a_re * a_re + a_im * a_im + l_re * l_re + l_im * l_im))
        return e_re, e_im, power

    sums = (zeros, zeros, zeros)
    beat(0, zh)
    send_lag(zh)
    beat(1, z_at(-1))
    send_lag(z_at(-1))
    sums = margin(zh, sums)
    beat(2, z_at(1))
    send_lag(z_at(1))
    sums = margin(z_at(-1), sums)
    relay.wait_recv()
    x_copies[3] = spread(3, z_at(2))
    sums = margin(z_at(1), sums)
    beat(3, z_at(2))
    send_lag(z_at(2))
    sums = margin(z_at(2), sums)

    lane = iota((1, 128), 1)
    own = jnp.where(lane == 3, count, 0.0)
    for k, v in enumerate(sums):
        own = jnp.where(lane == k, jnp.sum(jnp.sum(v, axis=0, keepdims=True), axis=1, keepdims=True), own)
    stat_out[0] = own

    def stat_copy(k):
        return remote(stat_out, stat_in.at[pl.ds(tiles - 1 - k, 1)], stat_send, stat_recv, lax.rem(t + k, tiles), d)

    for k in range(1, tiles):
        stat_copy(k).start()

    total = jnp.zeros((2 * rows_n, 128), F32)
    per = 128 // LR
    for m in range(chunks):
        pick = jnp.where(iota((128, 128), 1) == m * per + iota((128, 128), 0) // LR, 1.0 / (LA * LR), 0.0).astype(BF16)
        v = ifg[m]
        hi = v.astype(BF16)
        lo = (v - hi.astype(F32)).astype(BF16)
        total += jnp.dot(hi, pick, preferred_element_type=F32) + jnp.dot(lo, pick, preferred_element_type=F32)
    acc[...] = total
    pairs = [acc[pl.ds(first, rows_n, stride=LA), :] for first in range(LA)]
    both = functools.reduce(lambda a, b: a + b, pairs)
    looks_re, looks_im = both[: rows_n // LA], both[rows_n // LA :]

    pltpu.make_async_copy(stat_in, stat_in, stat_recv).wait()
    grand = own + jnp.sum(stat_in[...], axis=0)
    t_re, t_im, t_pow, t_cnt = (jnp.sum(jnp.where(lane == k, grand, 0.0), axis=1, keepdims=True) for k in range(4))
    magnitude = jnp.sqrt(t_re * t_re + t_im * t_im)
    floor_val = (t_pow + 1e-06) / jnp.sqrt(jnp.maximum(t_cnt, 1.0))
    denom = jnp.maximum(magnitude, floor_val)
    u_re = t_re / denom
    u_im = t_im / denom
    out[0, 0] = looks_re * u_re + looks_im * u_im
    out[0, 1] = looks_im * u_re - looks_re * u_im

    for copy in z_copies:
        copy.wait_send()
    relay.wait_send()
    for group in range(4):
        for copy in x_copies[group]:
            copy.wait_send()

    @pl.when(t < tiles - 1)
    def _():
        up.wait_send()

    @pl.when(t > 0)
    def _():
        down.wait_send()
        for z in range(nz):
            lag_copy(z).wait_send()

    pltpu.make_async_copy(stat_in, stat_in, stat_send).wait()


def solution(mesh):
    tiles, dates = mesh.shape["tile"], mesh.shape["date"]
    nz = dates // NX

    def shards(secondary, primary, margin_mask, az_off, rg_off, az_frac, rg_frac):
        rows_n, cols_n = secondary.shape[2:]
        width = primary.shape[2]
        any_ = pl.BlockSpec(memory_space=pl.ANY)
        vmem = pl.BlockSpec(memory_space=pltpu.VMEM)
        smem = pl.BlockSpec(memory_space=pltpu.SMEM)
        dma = pltpu.SemaphoreType.DMA
        chunks = cols_n // 128
        return pl.pallas_call(
            functools.partial(kernel, tiles, dates),
            out_shape=jax.ShapeDtypeStruct((1, 2, rows_n // LA, cols_n // LR), F32),
            in_specs=[any_, any_, vmem, smem, smem, smem, smem],
            out_specs=vmem,
            scratch_shapes=[
                pltpu.VMEM((2, rows_n + 2 * RIM, cols_n), BF16),
                pltpu.VMEM((2, rows_n, width), BF16),
                pltpu.VMEM((2 * rows_n, cols_n + 2 * SIDE), BF16),
                pltpu.VMEM((nz, NX, rows_n, 2 * width), BF16),
                pltpu.VMEM((chunks, 2 * rows_n, 128), BF16),
                pltpu.VMEM((chunks, 2 * rows_n, 128), F32),
                pltpu.VMEM((nz, NX // 2, 2, LAG, 128), BF16),
                pltpu.VMEM((nz, NX // 2, 2, LAG, 128), BF16),
                pltpu.VMEM((1, 1, 128), F32),
                pltpu.VMEM((tiles - 1, 1, 128), F32),
                pltpu.VMEM((2 * rows_n, 128), F32),
                dma((2,)), dma((2,)), dma((2,)), dma((3,)), dma((3,)),
                dma((4, NX - 1)), dma((4, NX - 1)), dma((nz,)), dma((nz,)), dma, dma,
            ],
            compiler_params=pltpu.CompilerParams(collective_id=0, has_side_effects=True),
            name="coregister",
        )(secondary, primary, margin_mask.reshape(1, rows_n), az_off, rg_off, az_frac, rg_frac)

    return jax.shard_map(
        shards,
        mesh=mesh,
        in_specs=(
            P("date", None, "tile", None),
            P(None, "tile", "date"),
            P("tile"),
            P("date", "tile"),
            P("date", "tile"),
            P("date", "tile"),
            P("date", "tile"),
        ),
        out_specs=P("date", None, "tile", None),
        check_vma=False,
    )
```

time: 182 us -> 45.6 us (0.25)
  blocking collectives: 116 us -> 0 us
  Pallas kernels: 0 us -> 39.8 us
  starting transfers between devices: 13.9 us -> 0 us
  waiting for transfers between devices: 12.3 us -> 0 us
  other arithmetic: 12 us -> 0 us
  local copies, waits for them, and re-layouts: 14.7 us -> 2.9 us
  between operations: 8.73 us -> 2.6 us
  matrix products: 3.52 us -> 0 us
    psum x1 -> x0, blocking collectives: 61 us -> none  [shards(): totals = lax.psum(stats, 'tile')]
    all_gather x1 -> x0, blocking collectives: 55.4 us -> none  [shards(): prim = lax.all_gather(primary, 'date', axis=2, tiled=True)[None]]
    pallas_call x0 -> x1, Pallas kernels: none -> 39.8 us  [shards(): pl.pallas_call(functools.partial(kernel, tiles, dates), out_shape=jax.Sha...]
    ppermute x3 -> x0, starting transfers between devices: 13.9 us -> none  [the longest x1 5.46 us: padded(): lax.ppermute(lax.slice_in_dim(block, 0, width, axis=dim), axis, backward)]
    ppermute x3 -> x0, waiting for transfers between devices: 12.3 us -> none  [the longest x1 12.3 us: passed_along(): lax.ppermute(value, axis, [(source, source + steps) for source in range(i...]
    reduce_sum x3 -> x0, other arithmetic: 8.34 us -> none  [the longest x2 7.34 us: multilook(): values.reshape(depth, rows_n // LA, LA, cols_n // LR, LR).mean(axis=(2, 4))]
    sub x1 -> x0, local copies, waits for them, and re-layouts: 4.97 us -> none  [shards(): c_im = multilook(ifg_im * u_re - ifg_re * u_im)]
    add x1 -> x0, local copies, waits for them, and re-layouts: 4.95 us -> none  [shards(): c_re = multilook(ifg_re * u_re + ifg_im * u_im)]
  transfers between devices with their start and end apart: 3 -> 0, of which waited for: 1 -> 0; matrix products, arithmetic and copies ran while one was open for 1% -> 0% of each run, Pallas kernels for 0% -> 0%
where the time goes in v1:
time: 45.6 us; the launch traced here: 45.3 us
  Pallas kernels  39.8 us (87%)
  local copies, waits for them, and re-layouts  2.9 us (6%)
  between operations  2.6 us (6%)
    pallas_call x1, Pallas kernels, shards(): pl.pallas_call(functools.partial(kernel, tiles, dates), out_shape=jax.Sha...  39.8 us
    unnamed x2, local copies, waits for them, and re-layouts  2.9 us

profile of v1, /device:TPU:1, one launch (start us, length us, event | category | flops | bytes accessed | tf_op | source)
XLA Modules:
  0.0 45.3 jit_solution(16536091493853047461)
XLA Ops:
  2.6 1.5 %copy.8.prim = bf16[2,96,64]{2,1,0:T(8,128)(2,1)} copy(bf16[2,96,64]{1,2,0:T(8,128)(2,1)} %param.8) | data formatting | bytes 49152 | tf_op args[1]
  4.1 39.8 %coregister.1 = f32[1,2,48,128]{3,2,1,0:T(8,128)} custom-call(bf16[1,2,96,1024]{3,2,1,0:T(8,128)(2,1)} %sec.1, bf16[2,96,64]{2,1,0:T(8,128)(2,1)} %copy.8.prim, s32[1,96]{1,0:T(1,128)} %bitcast.1, s32[1,1]{1,0:T(1,128)S(6)} %copy.10.az_off, s32[1,1]{1,0:T(1,128)S(6)} %copy.11.rg_off, f32[1,1]{1,0:T(1,128)S(6)} %copy.12.az_frac, f32[1,1]{1,0:T(1,128)S(6)} %copy.13.rg_frac), custom_call_target="tpu_custom_call" | custom-call | tf_op jit(solution)/shard_map/coregister/pallas_call | solution.py:310
  43.9 1.4 %copy.14 = f32[1,2,48,128]{3,2,1,0:T(8,128)} copy(f32[1,2,48,128]{3,2,1,0:T(8,128)} %coregister.1) | data formatting | bytes 98304

commit v2 on v1

--- a/solution.py
+++ b/solution.py
@@ -39,8 +39,9 @@
 
 def kernel(
     tiles, dates,
-    sec, prim, mask, az_off, rg_off, az_frac, rg_frac,
+    sec, prim, mask_at, az_off_at, rg_off_at, az_frac_at, rg_frac_at,
     out,
+    mask, az_off, rg_off, az_frac, rg_frac,
     ext, prim_in, azim, gath, res, ifg, lag_out, lag_in, stat_out, stat_in, acc,
     local_sem, halo_send, halo_recv, z_send, z_recv, x_send, x_recv,
     lag_send, lag_recv, stat_send, stat_recv,
@@ -48,7 +49,7 @@
     nz = dates // NX
     rows_n = sec.shape[2]
     cols_n = sec.shape[3]
-    width = prim.shape[2]
+    width = prim.shape[0] // 2
     chunks = cols_n // 128
     t = lax.axis_index("tile")
     d = lax.axis_index("date")
@@ -81,6 +82,14 @@
 
     prim_copy = pltpu.make_async_copy(prim, prim_in, local_sem.at[0])
     prim_copy.start()
+    small_copies = [
+        pltpu.make_async_copy(src, dst, local_sem.at[2 + k])
+        for k, (src, dst) in enumerate((
+            (az_off_at, az_off), (rg_off_at, rg_off), (az_frac_at, az_frac), (rg_frac_at, rg_frac), (mask_at, mask),
+        ))
+    ]
+    for copy in small_copies:
+        copy.start()
     own_copy = pltpu.make_async_copy(sec.at[0], ext.at[:, pl.ds(RIM, rows_n), :], local_sem.at[1])
     own_copy.start()
 
@@ -95,22 +104,7 @@
 
     prim_copy.wait()
     mine = gath.at[zh, x]
-    mine[:, pl.ds(0, width)] = prim_in[0]
-    mine[:, pl.ds(width, width)] = prim_in[1]
-
-    az_rows = tap_rows(az_frac[0, 0], 256)
-    rg_rows = tap_rows(rg_frac[0, 0], 256)
-    span = rows_n + 2 * RIM
-    az_taps = band(az_rows[:, :span], iota((rows_n, span), 1) - iota((rows_n, span), 0) - (az_off[0, 0] + RIM))
-    rg_shape = (BLOCK + 2 * SIDE, BLOCK)
-    rg_taps = band(rg_rows, iota(rg_shape, 0) - iota(rg_shape, 1) - (rg_off[0, 0] + SIDE))
-    azim[:, pl.ds(0, SIDE)] = jnp.zeros((2 * rows_n, SIDE), BF16)
-    azim[:, pl.ds(SIDE + cols_n, SIDE)] = jnp.zeros((2 * rows_n, SIDE), BF16)
-    lanes = iota((1, mask.shape[1]), 1)
-    marks = jnp.where(mask[...] != 0, 1.0, 0.0).astype(F32)
-    picked = iota((LAG, mask.shape[1]), 1) == iota((LAG, mask.shape[1]), 0) + (rows_n - LAG)
-    weight = jnp.sum(jnp.where(picked, marks, 0.0), axis=1, keepdims=True)
-    count = jnp.sum(marks, axis=1, keepdims=True) * float(cols_n)
+    mine[...] = prim_in[...].astype(F32).T.astype(BF16)
 
     pl.semaphore_wait(barrier, partners)
 
@@ -143,6 +137,22 @@
     @pl.when(t > 0)
     def _():
         down.start()
+
+    for copy in small_copies:
+        copy.wait()
+    az_rows = tap_rows(az_frac[...], 256)
+    rg_rows = tap_rows(rg_frac[...], 256)
+    span = rows_n + 2 * RIM
+    az_taps = band(az_rows[:, :span], iota((rows_n, span), 1) - iota((rows_n, span), 0) - (az_off[...] + RIM))
+    rg_shape = (BLOCK + 2 * SIDE, BLOCK)
+    rg_taps = band(rg_rows, iota(rg_shape, 0) - iota(rg_shape, 1) - (rg_off[...] + SIDE))
+    azim[:, pl.ds(0, SIDE)] = jnp.zeros((2 * rows_n, SIDE), BF16)
+    azim[:, pl.ds(SIDE + cols_n, SIDE)] = jnp.zeros((2 * rows_n, SIDE), BF16)
+    lanes = iota((1, mask.shape[1]), 1)
+    marks = jnp.where(mask[...] != 0, 1.0, 0.0).astype(F32)
+    picked = iota((LAG, mask.shape[1]), 1) == iota((LAG, mask.shape[1]), 0) + (rows_n - LAG)
+    weight = jnp.sum(jnp.where(picked, marks, 0.0), axis=1, keepdims=True)
+    count = jnp.sum(marks, axis=1, keepdims=True) * float(cols_n)
 
     own_copy.wait()
 
@@ -304,17 +314,19 @@
         width = primary.shape[2]
         any_ = pl.BlockSpec(memory_space=pl.ANY)
         vmem = pl.BlockSpec(memory_space=pltpu.VMEM)
-        smem = pl.BlockSpec(memory_space=pltpu.SMEM)
         dma = pltpu.SemaphoreType.DMA
         chunks = cols_n // 128
         return pl.pallas_call(
             functools.partial(kernel, tiles, dates),
-            out_shape=jax.ShapeDtypeStruct((1, 2, rows_n // LA, cols_n // LR), F32),
-            in_specs=[any_, any_, vmem, smem, smem, smem, smem],
+            out_shape=pltpu.VMEM((1, 2, rows_n // LA, cols_n // LR), F32),
+            in_specs=[any_] * 7,
             out_specs=vmem,
             scratch_shapes=[
+                pltpu.VMEM((1, rows_n), jnp.int32),
+                *[pltpu.VMEM((1, 1), jnp.int32)] * 2,
+                *[pltpu.VMEM((1, 1), F32)] * 2,
                 pltpu.VMEM((2, rows_n + 2 * RIM, cols_n), BF16),
-                pltpu.VMEM((2, rows_n, width), BF16),
+                pltpu.VMEM((2 * width, rows_n), BF16),
                 pltpu.VMEM((2 * rows_n, cols_n + 2 * SIDE), BF16),
                 pltpu.VMEM((nz, NX, rows_n, 2 * width), BF16),
                 pltpu.VMEM((chunks, 2 * rows_n, 128), BF16),
@@ -324,12 +336,12 @@
                 pltpu.VMEM((1, 1, 128), F32),
                 pltpu.VMEM((tiles - 1, 1, 128), F32),
                 pltpu.VMEM((2 * rows_n, 128), F32),
-                dma((2,)), dma((2,)), dma((2,)), dma((3,)), dma((3,)),
+                dma((7,)), dma((2,)), dma((2,)), dma((3,)), dma((3,)),
                 dma((4, NX - 1)), dma((4, NX - 1)), dma((nz,)), dma((nz,)), dma, dma,
             ],
             compiler_params=pltpu.CompilerParams(collective_id=0, has_side_effects=True),
             name="coregister",
-        )(secondary, primary, margin_mask.reshape(1, rows_n), az_off, rg_off, az_frac, rg_frac)
+        )(secondary, primary.transpose(0, 2, 1).reshape(2 * width, rows_n), margin_mask.reshape(1, rows_n), az_off, rg_off, az_frac, rg_frac)
 
     return jax.shard_map(
         shards,

time: 45.6 us -> 42 us (0.921)
  local copies, waits for them, and re-layouts: 2.9 us -> 0.62 us
  Pallas kernels: 39.8 us -> 38.6 us
    unnamed x2 -> x1, local copies, waits for them, and re-layouts: 2.9 us -> 0.62 us
    pallas_call x1, Pallas kernels: 39.8 us -> 38.6 us  [shards(): pl.pallas_call(functools.partial(kernel, tiles, dates), out_shape=pltpu.V...]
where the time goes in v2:
time: 42 us; the launch traced here: 41.8 us
  Pallas kernels  38.6 us (92%)
  between operations  2.59 us (6%)
  local copies, waits for them, and re-layouts  0.62 us (1%)
    pallas_call x1, Pallas kernels, shards(): pl.pallas_call(functools.partial(kernel, tiles, dates), out_shape=pltpu.V...  38.6 us

profile of v2, /device:TPU:1, one launch (start us, length us, event | category | flops | bytes accessed | tf_op | source)
XLA Modules:
  0.0 41.8 jit_solution(14661782587713671657)
XLA Ops:
  2.6 38.6 %coregister.1 = f32[1,2,48,128]{3,2,1,0:T(8,128)S(1)} custom-call(bf16[1,2,96,1024]{3,2,1,0:T(8,128)(2,1)} %sec.1, bf16[128,96]{1,0:T(8,128)(2,1)} %bitcast.4, s32[1,96]{1,0:T(1,128)} %bitcast.5, s32[1,1]{1,0:T(1,128)S(6)} %copy.10.az_off_at, s32[1,1]{1,0:T(1,128)S(6)} %copy.11.rg_off_at, f32[1,1]{1,0:T(1,128)S(6)} %copy.12.az_frac_at, ...), custom_call_target="tpu_custom_call" | custom-call | tf_op jit(solution)/shard_map/coregister/pallas_call | solution.py:319
  41.2 0.6 %copy.9 = f32[1,2,48,128]{3,2,1,0:T(8,128)} copy(f32[1,2,48,128]{3,2,1,0:T(8,128)S(1)} %coregister.1) | data formatting | bytes 98304

commit v3 on v2

--- a/solution.py
+++ b/solution.py
@@ -15,6 +15,7 @@
 SIDE = 128
 BLOCK = 256
 MESH = pl.DeviceIdType.MESH
+ROUNDS = (1, 2, 4, 8, 16)
 F32 = jnp.float32
 BF16 = jnp.bfloat16
 
@@ -45,6 +46,7 @@
     ext, prim_in, azim, gath, res, ifg, lag_out, lag_in, stat_out, stat_in, acc,
     local_sem, halo_send, halo_recv, z_send, z_recv, x_send, x_recv,
     lag_send, lag_recv, stat_send, stat_recv,
+    z_ready, x_ready, tile_ready, round_ready,
 ):
     nz = dates // NX
     rows_n = sec.shape[2]
@@ -54,10 +56,9 @@
     t = lax.axis_index("tile")
     d = lax.axis_index("date")
     zh, x = d // NX, lax.rem(d, NX)
-    step = 1 - 2 * lax.rem(t, 2)
 
     def z_at(k):
-        return lax.rem(zh + k * step + 2 * nz, nz)
+        return lax.rem(zh + k + nz, nz)
 
     def date_at(z, xx):
         return z * NX + xx
@@ -68,20 +69,31 @@
             device_id={"tile": tile, "date": date}, device_id_type=MESH,
         )
 
+    def order(z):
+        return jnp.where(z >= 2, 5 - z, z)
+
+    def x_at(k):
+        return lax.rem(x + k, NX)
+
+    def signal(sem, tile, date):
+        pl.semaphore_signal(sem, inc=1, device_id={"tile": tile, "date": date}, device_id_type=MESH)
+
+    z_first = {k: order(zh) < order(z_at(k)) for k in range(1, nz)}
+    x_first = {k: x < x_at(k) for k in range(1, NX)}
     barrier = pltpu.get_barrier_semaphore()
-    partners = 0
+    for k in range(1, nz):
+        @pl.when(z_first[k])
+        def _(k=k):
+            signal(barrier, t, date_at(z_at(k), x))
     for k in range(1, NX):
-        pl.semaphore_signal(barrier, inc=1, device_id={"tile": t, "date": date_at(zh, lax.rem(x + k, NX))}, device_id_type=MESH)
-        partners += 1
-    for k in (1, -1):
-        pl.semaphore_signal(barrier, inc=1, device_id={"tile": t, "date": date_at(z_at(k), x)}, device_id_type=MESH)
-        partners += 1
-    for k in range(1, tiles):
-        pl.semaphore_signal(barrier, inc=1, device_id={"tile": lax.rem(t + k, tiles), "date": d}, device_id_type=MESH)
-        partners += 1
-
-    prim_copy = pltpu.make_async_copy(prim, prim_in, local_sem.at[0])
-    prim_copy.start()
+        @pl.when(x_first[k])
+        def _(k=k):
+            signal(barrier, t, date_at(zh, x_at(k)))
+
+    @pl.when(t < tiles - 1)
+    def _():
+        signal(barrier, t + 1, d)
+
     small_copies = [
         pltpu.make_async_copy(src, dst, local_sem.at[2 + k])
         for k, (src, dst) in enumerate((
@@ -90,6 +102,8 @@
     ]
     for copy in small_copies:
         copy.start()
+    prim_copy = pltpu.make_async_copy(prim, prim_in, local_sem.at[0])
+    prim_copy.start()
     own_copy = pltpu.make_async_copy(sec.at[0], ext.at[:, pl.ds(RIM, rows_n), :], local_sem.at[1])
     own_copy.start()
 
@@ -106,37 +120,93 @@
     mine = gath.at[zh, x]
     mine[...] = prim_in[...].astype(F32).T.astype(BF16)
 
-    pl.semaphore_wait(barrier, partners)
-
-    z_copies = [
-        remote(mine, mine, z_send.at[0], z_recv.at[0], t, date_at(z_at(1), x)),
-        remote(mine, mine, z_send.at[1], z_recv.at[1], t, date_at(z_at(-1), x)),
-    ]
-    z_copies[0].start()
-    z_copies[1].start()
-
-    def spread(group, z):
+    before = order(zh) + x + jnp.where(t > 0, 1, 0)
+
+    @pl.when(before > 0)
+    def _():
+        pl.semaphore_wait(barrier, before)
+
+    for k in range(1, nz):
+        @pl.when(jnp.logical_not(z_first[k]))
+        def _(k=k):
+            signal(z_ready.at[nz - k - 1], t, date_at(z_at(k), x))
+    for k in range(1, NX):
+        @pl.when(jnp.logical_not(x_first[k]))
+        def _(k=k):
+            signal(x_ready.at[NX - k - 1], t, date_at(zh, x_at(k)))
+
+    @pl.when(t > 0)
+    def _():
+        signal(tile_ready, t - 1, d)
+
+    z_copies = {
+        k: remote(mine, mine, z_send.at[k - 1], z_recv.at[nz - k - 1], t, date_at(z_at(k), x))
+        for k in range(1, nz)
+    }
+
+    def x_copy(group, z, k):
         block = gath.at[z, x]
-        copies = [
-            remote(block, block, x_send.at[group, k - 1], x_recv.at[group, k - 1], t, date_at(zh, lax.rem(x + k, NX)))
-            for k in (2, 1, 3)
-        ]
-        for copy in copies:
-            copy.start()
-        return copies
-
-    x_copies = {0: spread(0, zh)}
+        return remote(block, block, x_send.at[group, k - 1], x_recv.at[group, k - 1], t, date_at(zh, x_at(k)))
+
+    for k in (2, 1, 3):
+        @pl.when(jnp.logical_not(z_first[k]))
+        def _(k=k):
+            z_copies[k].start()
+    for k in (2, 1, 3):
+        @pl.when(jnp.logical_not(x_first[k]))
+        def _(k=k):
+            x_copy(0, zh, k).start()
 
     up = remote(sec.at[0, :, pl.ds(rows_n - RIM, RIM), :], ext.at[:, pl.ds(0, RIM), :], halo_send.at[0], halo_recv.at[0], lax.rem(t + 1, tiles), d)
     down = remote(sec.at[0, :, pl.ds(0, RIM), :], ext.at[:, pl.ds(RIM + rows_n, RIM), :], halo_send.at[1], halo_recv.at[1], lax.rem(t + tiles - 1, tiles), d)
 
+    @pl.when(t > 0)
+    def _():
+        down.start()
+
+    for k in (1, 2, 3):
+        @pl.when(x_first[k])
+        def _(k=k):
+            pl.semaphore_wait(x_ready.at[k - 1], 1)
+            x_copy(0, zh, k).start()
+
     @pl.when(t < tiles - 1)
     def _():
+        pl.semaphore_wait(tile_ready, 1)
         up.start()
 
-    @pl.when(t > 0)
-    def _():
-        down.start()
+    def round_signal(i):
+        @pl.when(t >= ROUNDS[i])
+        def _():
+            signal(round_ready.at[i], t - ROUNDS[i], d)
+
+        @pl.when(t < tiles - ROUNDS[i])
+        def _():
+            signal(round_ready.at[i], t + ROUNDS[i], d)
+
+    def round_wait(i):
+        expected = jnp.where(t >= ROUNDS[i], 1, 0) + jnp.where(t < tiles - ROUNDS[i], 1, 0)
+
+        @pl.when(expected > 0)
+        def _():
+            pl.semaphore_wait(round_ready.at[i], expected)
+
+    def spread(group, z):
+        for k in (2, 1, 3):
+            x_copy(group, z, k).start()
+
+    def turn(k):
+        @pl.when(z_first[k])
+        def _():
+            pl.semaphore_wait(z_ready.at[k - 1], 1)
+            z_copies[k].start()
+
+    def arrive(k):
+        block = gath.at[z_at(k), x]
+        remote(block, block, z_send.at[k - 1], z_recv.at[k - 1], t, date_at(z_at(k), x)).wait_recv()
+        spread(k, z_at(k))
+
+    round_signal(0)
 
     for copy in small_copies:
         copy.wait()
@@ -169,13 +239,8 @@
             part = jnp.dot(az_taps, ext[plane, :, pl.ds(b * BLOCK, BLOCK)], preferred_element_type=F32)
             azim[pl.ds(plane * rows_n, rows_n), pl.ds(SIDE + b * BLOCK, BLOCK)] = part.astype(BF16)
 
-    near = gath.at[z_at(-1), x]
-    z_copies[0].wait_recv()
-    relay = remote(near, near, z_send.at[2], z_recv.at[2], t, date_at(z_at(1), x))
-    relay.start()
-    x_copies[1] = spread(1, z_at(-1))
-    z_copies[1].wait_recv()
-    x_copies[2] = spread(2, z_at(1))
+    round_wait(0)
+    round_signal(1)
 
     for b in range(cols_n // BLOCK):
         part = jnp.dot(azim[:, pl.ds(b * BLOCK, BLOCK + 2 * SIDE)], rg_taps, preferred_element_type=F32).astype(BF16)
@@ -183,11 +248,23 @@
             half = part[:, h * 128 : (h + 1) * 128]
             res[b * (BLOCK // 128) + h] = half
 
+    round_wait(1)
+    round_signal(2)
+    turn(1)
+    arrive(1)
+    round_wait(2)
+    round_signal(3)
+    turn(3)
+    arrive(3)
+    round_wait(3)
+    round_signal(4)
+    turn(2)
+
     low_half = iota((rows_n, 128), 1) < width
 
     def beat(group, z):
-        for copy in x_copies[group]:
-            copy.wait_recv()
+        for k in range(1, NX):
+            x_copy(group, z, k).wait_recv()
         for q in range(NX // 2):
             m = z * (NX // 2) + q
             a = gath[z, 2 * q].astype(F32)
@@ -236,17 +313,17 @@
     sums = (zeros, zeros, zeros)
     beat(0, zh)
     send_lag(zh)
-    beat(1, z_at(-1))
-    send_lag(z_at(-1))
+    beat(1, z_at(1))
+    send_lag(z_at(1))
     sums = margin(zh, sums)
-    beat(2, z_at(1))
-    send_lag(z_at(1))
-    sums = margin(z_at(-1), sums)
-    relay.wait_recv()
-    x_copies[3] = spread(3, z_at(2))
+    beat(3, z_at(3))
+    send_lag(z_at(3))
     sums = margin(z_at(1), sums)
-    beat(3, z_at(2))
+    arrive(2)
+    sums = margin(z_at(3), sums)
+    beat(2, z_at(2))
     send_lag(z_at(2))
+    round_wait(4)
     sums = margin(z_at(2), sums)
 
     lane = iota((1, 128), 1)
@@ -285,12 +362,11 @@
     out[0, 0] = looks_re * u_re + looks_im * u_im
     out[0, 1] = looks_im * u_re - looks_re * u_im
 
-    for copy in z_copies:
-        copy.wait_send()
-    relay.wait_send()
-    for group in range(4):
-        for copy in x_copies[group]:
-            copy.wait_send()
+    for k in range(1, nz):
+        z_copies[k].wait_send()
+    for group in range(nz):
+        for k in range(1, NX):
+            x_copy(group, z_at(group), k).wait_send()
 
     @pl.when(t < tiles - 1)
     def _():
@@ -312,14 +388,15 @@
     def shards(secondary, primary, margin_mask, az_off, rg_off, az_frac, rg_frac):
         rows_n, cols_n = secondary.shape[2:]
         width = primary.shape[2]
-        any_ = pl.BlockSpec(memory_space=pl.ANY)
+        hbm = pl.BlockSpec(memory_space=pltpu.HBM)
         vmem = pl.BlockSpec(memory_space=pltpu.VMEM)
         dma = pltpu.SemaphoreType.DMA
+        regular = pltpu.SemaphoreType.REGULAR
         chunks = cols_n // 128
         return pl.pallas_call(
             functools.partial(kernel, tiles, dates),
             out_shape=pltpu.VMEM((1, 2, rows_n // LA, cols_n // LR), F32),
-            in_specs=[any_] * 7,
+            in_specs=[hbm] * 7,
             out_specs=vmem,
             scratch_shapes=[
                 pltpu.VMEM((1, rows_n), jnp.int32),
@@ -338,6 +415,7 @@
                 pltpu.VMEM((2 * rows_n, 128), F32),
                 dma((7,)), dma((2,)), dma((2,)), dma((3,)), dma((3,)),
                 dma((4, NX - 1)), dma((4, NX - 1)), dma((nz,)), dma((nz,)), dma, dma,
+                regular((nz - 1,)), regular((NX - 1,)), regular, regular((len(ROUNDS),)),
             ],
             compiler_params=pltpu.CompilerParams(collective_id=0, has_side_effects=True),
             name="coregister",

time: 42 us -> 41.7 us (level); the launches traced: 41.8 us -> 40.9 us
  Pallas kernels: 38.6 us -> 37.7 us
    pallas_call x1, Pallas kernels: 38.6 us -> 37.7 us  [shards(): pl.pallas_call(functools.partial(kernel, tiles, dates), out_shape=pltpu.V...]
where the time goes in v3:
time: 41.7 us; the launch traced here: 40.9 us
  Pallas kernels  37.7 us (90%)
  between operations  2.59 us (6%)
  local copies, waits for them, and re-layouts  0.62 us (1%)
    pallas_call x1, Pallas kernels, shards(): pl.pallas_call(functools.partial(kernel, tiles, dates), out_shape=pltpu.V...  37.7 us

profile of v3, /device:TPU:1, one launch (start us, length us, event | category | flops | bytes accessed | tf_op | source)
XLA Modules:
  0.0 40.9 jit_solution(2040185956262922239)
XLA Ops:
  2.6 37.7 %coregister.1 = f32[1,2,48,128]{3,2,1,0:T(8,128)S(1)} custom-call(bf16[1,2,96,1024]{3,2,1,0:T(8,128)(2,1)} %sec.1, bf16[128,96]{1,0:T(8,128)(2,1)} %bitcast.4, s32[1,96]{1,0:T(1,128)} %bitcast.5, s32[1,1]{1,0:T(1,128)S(6)} %copy.10.az_off_at, s32[1,1]{1,0:T(1,128)S(6)} %copy.11.rg_off_at, f32[1,1]{1,0:T(1,128)S(6)} %copy.12.az_frac_at, ...), custom_call_target="tpu_custom_call" | custom-call | tf_op jit(solution)/shard_map/coregister/pallas_call | solution.py:396
  40.3 0.6 %copy.9 = f32[1,2,48,128]{3,2,1,0:T(8,128)} copy(f32[1,2,48,128]{3,2,1,0:T(8,128)S(1)} %coregister.1) | data formatting | bytes 98304

commit v4 on v3

--- a/solution.py
+++ b/solution.py
@@ -43,9 +43,9 @@
     sec, prim, mask_at, az_off_at, rg_off_at, az_frac_at, rg_frac_at,
     out,
     mask, az_off, rg_off, az_frac, rg_frac,
-    ext, prim_in, azim, gath, res, ifg, lag_out, lag_in, stat_out, stat_in, acc,
+    ext, prim_in, azim, gath, res, ifg, gnext, rnext, stat_out, stat_in, acc,
     local_sem, halo_send, halo_recv, z_send, z_recv, x_send, x_recv,
-    lag_send, lag_recv, stat_send, stat_recv,
+    next_send, next_recv, row_send, row_recv, stat_send, stat_recv,
     z_ready, x_ready, tile_ready, round_ready,
 ):
     nz = dates // NX
@@ -114,7 +114,8 @@
     @pl.when(t == tiles - 1)
     def _():
         ext[:, pl.ds(RIM + rows_n, RIM), :] = jnp.zeros((2, RIM, cols_n), BF16)
-        lag_in[...] = jnp.zeros(lag_in.shape, BF16)
+        gnext[...] = jnp.zeros(gnext.shape, BF16)
+        rnext[...] = jnp.zeros(rnext.shape, BF16)
 
     prim_copy.wait()
     mine = gath.at[zh, x]
@@ -126,7 +127,7 @@
     def _():
         pl.semaphore_wait(barrier, before)
 
-    for k in range(1, nz):
+    for k in (1, nz - 1):
         @pl.when(jnp.logical_not(z_first[k]))
         def _(k=k):
             signal(z_ready.at[nz - k - 1], t, date_at(z_at(k), x))
@@ -164,11 +165,12 @@
     def _():
         down.start()
 
-    for k in (1, 2, 3):
+    for k in range(1, NX):
         @pl.when(x_first[k])
         def _(k=k):
             pl.semaphore_wait(x_ready.at[k - 1], 1)
             x_copy(0, zh, k).start()
+            signal(x_ready.at[NX - k - 1], t, date_at(zh, x_at(k)))
 
     @pl.when(t < tiles - 1)
     def _():
@@ -191,7 +193,20 @@
         def _():
             pl.semaphore_wait(round_ready.at[i], expected)
 
+    def next_copy(group, z, k):
+        return remote(
+            gath.at[z, x, pl.ds(0, LAG), :], gnext.at[z, x], next_send.at[group, k], next_recv.at[group, k],
+            lax.rem(t + tiles - 1, tiles), date_at(zh, x_at(k)),
+        )
+
+    def spread_back(group, z):
+        @pl.when(t > 0)
+        def _():
+            for k in (2, 1, 3, 0):
+                next_copy(group, z, k).start()
+
     def spread(group, z):
+        spread_back(group, z)
         for k in (2, 1, 3):
             x_copy(group, z, k).start()
 
@@ -205,6 +220,16 @@
         block = gath.at[z_at(k), x]
         remote(block, block, z_send.at[k - 1], z_recv.at[k - 1], t, date_at(z_at(k), x)).wait_recv()
         spread(k, z_at(k))
+
+    def pass_on(of, to):
+        block = gath.at[z_at(of), x]
+        return remote(block, block, z_send.at[1], z_recv.at[1], t, date_at(z_at(to), x))
+
+    for k in range(1, NX):
+        @pl.when(jnp.logical_not(x_first[k]))
+        def _(k=k):
+            pl.semaphore_wait(x_ready.at[k - 1], 1)
+    spread_back(0, zh)
 
     round_signal(0)
 
@@ -248,83 +273,87 @@
             half = part[:, h * 128 : (h + 1) * 128]
             res[b * (BLOCK // 128) + h] = half
 
+    def row_copy(plane):
+        return remote(
+            res.at[:, pl.ds(plane * rows_n, LAG), :], rnext.at[plane], row_send.at[plane], row_recv.at[plane],
+            lax.rem(t + tiles - 1, tiles), d,
+        )
+
     round_wait(1)
     round_signal(2)
+
+    @pl.when(t > 0)
+    def _():
+        row_copy(0).start()
+        row_copy(1).start()
+
     turn(1)
     arrive(1)
     round_wait(2)
     round_signal(3)
     turn(3)
+
+    @pl.when(zh == 0)
+    def _():
+        pass_on(1, 3).start()
+
     arrive(3)
+
+    @pl.when(zh == 1)
+    def _():
+        pass_on(3, 1).start()
+
     round_wait(3)
     round_signal(4)
-    turn(2)
+
+    @pl.when(t < tiles - 1)
+    def _():
+        row_copy(0).wait_recv()
+        row_copy(1).wait_recv()
 
     low_half = iota((rows_n, 128), 1) < width
 
-    def beat(group, z):
+    def product(block_of, z, q, r_re, r_im, low):
+        a = block_of[z, 2 * q].astype(F32)
+        b = block_of[z, 2 * q + 1].astype(F32)
+        p_re = jnp.where(low, a, pltpu.roll(b, width, 1))
+        p_im = jnp.where(low, pltpu.roll(a, width, 1), b)
+        return p_re * r_re + p_im * r_im, p_im * r_re - p_re * r_im
+
+    def fold(v):
+        return jnp.sum(v.reshape(LAG // 8, 8, 128), axis=0)
+
+    def beat(group, z, sums):
         for k in range(1, NX):
             x_copy(group, z, k).wait_recv()
-        for q in range(NX // 2):
-            m = z * (NX // 2) + q
-            a = gath[z, 2 * q].astype(F32)
-            b = gath[z, 2 * q + 1].astype(F32)
-            p_re = jnp.where(low_half, a, pltpu.roll(b, width, 1))
-            p_im = jnp.where(low_half, pltpu.roll(a, width, 1), b)
-            r_re = res[m, pl.ds(0, rows_n)].astype(F32)
-            r_im = res[m, pl.ds(rows_n, rows_n)].astype(F32)
-            i_re = p_re * r_re + p_im * r_im
-            i_im = p_im * r_re - p_re * r_im
-            ifg[m, pl.ds(0, rows_n)] = i_re
-            ifg[m, pl.ds(rows_n, rows_n)] = i_im
-            lag_out[z, q, 0] = i_re[:LAG].astype(BF16)
-            lag_out[z, q, 1] = i_im[:LAG].astype(BF16)
-
-    def lag_copy(z):
-        return remote(lag_out.at[z], lag_in.at[z], lag_send.at[z], lag_recv.at[z], lax.rem(t + tiles - 1, tiles), d)
-
-    def send_lag(z):
-        @pl.when(t > 0)
-        def _():
-            lag_copy(z).start()
-
-    zeros = jnp.zeros((8, 128), F32)
-
-    def fold(v):
-        return jnp.sum(v.reshape(LAG // 8, 8, 128), axis=0)
-
-    def margin(z, sums):
+
         @pl.when(t < tiles - 1)
         def _():
-            lag_copy(z).wait_recv()
+            for k in range(NX):
+                next_copy(group, z, k).wait_recv()
 
         e_re, e_im, power = sums
         for q in range(NX // 2):
             m = z * (NX // 2) + q
-            a_re = ifg[m, pl.ds(rows_n - LAG, LAG)]
-            a_im = ifg[m, pl.ds(2 * rows_n - LAG, LAG)]
-            l_re = lag_in[z, q, 0].astype(F32)
-            l_im = lag_in[z, q, 1].astype(F32)
+            i_re, i_im = product(
+                gath, z, q, res[m, pl.ds(0, rows_n)].astype(F32), res[m, pl.ds(rows_n, rows_n)].astype(F32), low_half
+            )
+            ifg[m, pl.ds(0, rows_n)] = i_re
+            ifg[m, pl.ds(rows_n, rows_n)] = i_im
+            l_re, l_im = product(gnext, z, q, rnext[0, m].astype(F32), rnext[1, m].astype(F32), low_half[:LAG])
+            a_re, a_im = i_re[rows_n - LAG :], i_im[rows_n - LAG :]
             e_re += fold(weight * (a_re * l_re + a_im * l_im))
             e_im += fold(weight * (a_im * l_re - a_re * l_im))
             power += fold((0.5 * weight) * (a_re * a_re + a_im * a_im + l_re * l_re + l_im * l_im))
         return e_re, e_im, power
 
-    sums = (zeros, zeros, zeros)
-    beat(0, zh)
-    send_lag(zh)
-    beat(1, z_at(1))
-    send_lag(z_at(1))
-    sums = margin(zh, sums)
-    beat(3, z_at(3))
-    send_lag(z_at(3))
-    sums = margin(z_at(1), sums)
+    zeros = jnp.zeros((8, 128), F32)
+    sums = beat(0, zh, (zeros, zeros, zeros))
+    sums = beat(1, z_at(1), sums)
+    sums = beat(3, z_at(3), sums)
+    round_wait(4)
     arrive(2)
-    sums = margin(z_at(3), sums)
-    beat(2, z_at(2))
-    send_lag(z_at(2))
-    round_wait(4)
-    sums = margin(z_at(2), sums)
+    sums = beat(2, z_at(2), sums)
 
     lane = iota((1, 128), 1)
     own = jnp.where(lane == 3, count, 0.0)
@@ -375,8 +404,11 @@
     @pl.when(t > 0)
     def _():
         down.wait_send()
-        for z in range(nz):
-            lag_copy(z).wait_send()
+        for group in range(nz):
+            for k in range(NX):
+                next_copy(group, z_at(group), k).wait_send()
+        row_copy(0).wait_send()
+        row_copy(1).wait_send()
 
     pltpu.make_async_copy(stat_in, stat_in, stat_send).wait()
 
@@ -408,13 +440,13 @@
                 pltpu.VMEM((nz, NX, rows_n, 2 * width), BF16),
                 pltpu.VMEM((chunks, 2 * rows_n, 128), BF16),
                 pltpu.VMEM((chunks, 2 * rows_n, 128), F32),
-                pltpu.VMEM((nz, NX // 2, 2, LAG, 128), BF16),
-                pltpu.VMEM((nz, NX // 2, 2, LAG, 128), BF16),
+                pltpu.VMEM((nz, NX, LAG, 2 * width), BF16),
+                pltpu.VMEM((2, chunks, LAG, 128), BF16),
                 pltpu.VMEM((1, 1, 128), F32),
                 pltpu.VMEM((tiles - 1, 1, 128), F32),
                 pltpu.VMEM((2 * rows_n, 128), F32),
                 dma((7,)), dma((2,)), dma((2,)), dma((3,)), dma((3,)),
-                dma((4, NX - 1)), dma((4, NX - 1)), dma((nz,)), dma((nz,)), dma, dma,
+                dma((nz, NX - 1)), dma((nz, NX - 1)), dma((nz, NX)), dma((nz, NX)), dma((2,)), dma((2,)), dma, dma,
                 regular((nz - 1,)), regular((NX - 1,)), regular, regular((len(ROUNDS),)),
             ],
             compiler_params=pltpu.CompilerParams(collective_id=0, has_side_effects=True),

time: 41.7 us -> 41 us (0.983)
  the two profiles are of different devices: /device:TPU:1 before, /device:TPU:352 now
where the time goes in v4:
time: 41 us; the launch traced here: 40.8 us
  Pallas kernels  37.6 us (92%)
  between operations  2.59 us (6%)
  local copies, waits for them, and re-layouts  0.62 us (2%)
    pallas_call x1, Pallas kernels, shards(): pl.pallas_call(functools.partial(kernel, tiles, dates), out_shape=pltpu.V...  37.6 us

profile of v4, /device:TPU:352, one launch (start us, length us, event | category | flops | bytes accessed | tf_op | source)
XLA Modules:
  0.0 40.8 jit_solution(938484418810801426)
XLA Ops:
  2.6 37.6 %coregister.1 = f32[1,2,48,128]{3,2,1,0:T(8,128)S(1)} custom-call(bf16[1,2,96,1024]{3,2,1,0:T(8,128)(2,1)} %sec.1, bf16[128,96]{1,0:T(8,128)(2,1)} %bitcast.4, s32[1,96]{1,0:T(1,128)} %bitcast.5, s32[1,1]{1,0:T(1,128)S(6)} %copy.10.az_off_at, s32[1,1]{1,0:T(1,128)S(6)} %copy.11.rg_off_at, f32[1,1]{1,0:T(1,128)S(6)} %copy.12.az_frac_at, ...), custom_call_target="tpu_custom_call" | custom-call | tf_op jit(solution)/shard_map/coregister/pallas_call | solution.py:428
  40.2 0.6 %copy.9 = f32[1,2,48,128]{3,2,1,0:T(8,128)} copy(f32[1,2,48,128]{3,2,1,0:T(8,128)S(1)} %coregister.1) | data formatting | bytes 98304

commit v5 on v4

--- a/solution.py
+++ b/solution.py
@@ -288,15 +288,15 @@
         row_copy(1).start()
 
     turn(1)
+    turn(3)
     arrive(1)
+
+    @pl.when(zh == 0)
+    def _():
+        pass_on(1, 3).start()
+
     round_wait(2)
     round_signal(3)
-    turn(3)
-
-    @pl.when(zh == 0)
-    def _():
-        pass_on(1, 3).start()
-
     arrive(3)
 
     @pl.when(zh == 1)
@@ -305,6 +305,7 @@
 
     round_wait(3)
     round_signal(4)
+    arrive(2)
 
     @pl.when(t < tiles - 1)
     def _():
@@ -352,7 +353,6 @@
     sums = beat(1, z_at(1), sums)
     sums = beat(3, z_at(3), sums)
     round_wait(4)
-    arrive(2)
     sums = beat(2, z_at(2), sums)
 
     lane = iota((1, 128), 1)

time: 41 us -> 37.2 us (0.907)
  the two profiles are of different devices: /device:TPU:352 before, /device:TPU:1 now
where the time goes in v5:
time: 37.2 us; the launch traced here: 37 us
  Pallas kernels  33.8 us (91%)
  between operations  2.59 us (7%)
  local copies, waits for them, and re-layouts  0.62 us (2%)
    pallas_call x1, Pallas kernels, shards(): pl.pallas_call(functools.partial(kernel, tiles, dates), out_shape=pltpu.V...  33.8 us

profile of v5, /device:TPU:1, one launch (start us, length us, event | category | flops | bytes accessed | tf_op | source)
XLA Modules:
  0.0 37.0 jit_solution(11482162261618289027)
XLA Ops:
  2.6 33.8 %coregister.1 = f32[1,2,48,128]{3,2,1,0:T(8,128)S(1)} custom-call(bf16[1,2,96,1024]{3,2,1,0:T(8,128)(2,1)} %sec.1, bf16[128,96]{1,0:T(8,128)(2,1)} %bitcast.4, s32[1,96]{1,0:T(1,128)} %bitcast.5, s32[1,1]{1,0:T(1,128)S(6)} %copy.10.az_off_at, s32[1,1]{1,0:T(1,128)S(6)} %copy.11.rg_off_at, f32[1,1]{1,0:T(1,128)S(6)} %copy.12.az_frac_at, ...), custom_call_target="tpu_custom_call" | custom-call | tf_op jit(solution)/shard_map/coregister/pallas_call | solution.py:428
  36.4 0.6 %copy.9 = f32[1,2,48,128]{3,2,1,0:T(8,128)} copy(f32[1,2,48,128]{3,2,1,0:T(8,128)S(1)} %coregister.1) | data formatting | bytes 98304

commit v6 on v5

--- a/solution.py
+++ b/solution.py
@@ -78,10 +78,14 @@
     def signal(sem, tile, date):
         pl.semaphore_signal(sem, inc=1, device_id={"tile": tile, "date": date}, device_id_type=MESH)
 
-    z_first = {k: order(zh) < order(z_at(k)) for k in range(1, nz)}
+    z_first = {k: order(zh) < order(z_at(k)) for k in (1, nz - 1)}
     x_first = {k: x < x_at(k) for k in range(1, NX)}
     barrier = pltpu.get_barrier_semaphore()
-    for k in range(1, nz):
+    @pl.when(zh == 0)
+    def _():
+        signal(barrier, t, date_at(z_at(2), x))
+
+    for k in (1, nz - 1):
         @pl.when(z_first[k])
         def _(k=k):
             signal(barrier, t, date_at(z_at(k), x))
@@ -117,11 +121,9 @@
         gnext[...] = jnp.zeros(gnext.shape, BF16)
         rnext[...] = jnp.zeros(rnext.shape, BF16)
 
-    prim_copy.wait()
     mine = gath.at[zh, x]
-    mine[...] = prim_in[...].astype(F32).T.astype(BF16)
-
-    before = order(zh) + x + jnp.where(t > 0, 1, 0)
+
+    before = sum(jnp.where(z_first[k], 0, 1) for k in (1, nz - 1)) + jnp.where(zh == 2, 1, 0) + x + jnp.where(t > 0, 1, 0)
 
     @pl.when(before > 0)
     def _():
@@ -140,16 +142,32 @@
     def _():
         signal(tile_ready, t - 1, d)
 
+    up = remote(sec.at[0, :, pl.ds(rows_n - RIM, RIM), :], ext.at[:, pl.ds(0, RIM), :], halo_send.at[0], halo_recv.at[0], lax.rem(t + 1, tiles), d)
+    down = remote(sec.at[0, :, pl.ds(0, RIM), :], ext.at[:, pl.ds(RIM + rows_n, RIM), :], halo_send.at[1], halo_recv.at[1], lax.rem(t + tiles - 1, tiles), d)
+
+    @pl.when(t > 0)
+    def _():
+        down.start()
+
+    prim_copy.wait()
+    mine[...] = prim_in[...].astype(F32).T.astype(BF16)
+
     z_copies = {
         k: remote(mine, mine, z_send.at[k - 1], z_recv.at[nz - k - 1], t, date_at(z_at(k), x))
-        for k in range(1, nz)
+        for k in (1, nz - 1)
     }
 
     def x_copy(group, z, k):
         block = gath.at[z, x]
         return remote(block, block, x_send.at[group, k - 1], x_recv.at[group, k - 1], t, date_at(zh, x_at(k)))
 
-    for k in (2, 1, 3):
+    direct = remote(mine, mine, z_send.at[1], z_recv.at[1], t, date_at(z_at(2), x))
+
+    @pl.when(zh == 2)
+    def _():
+        direct.start()
+
+    for k in (1, nz - 1):
         @pl.when(jnp.logical_not(z_first[k]))
         def _(k=k):
             z_copies[k].start()
@@ -157,13 +175,6 @@
         @pl.when(jnp.logical_not(x_first[k]))
         def _(k=k):
             x_copy(0, zh, k).start()
-
-    up = remote(sec.at[0, :, pl.ds(rows_n - RIM, RIM), :], ext.at[:, pl.ds(0, RIM), :], halo_send.at[0], halo_recv.at[0], lax.rem(t + 1, tiles), d)
-    down = remote(sec.at[0, :, pl.ds(0, RIM), :], ext.at[:, pl.ds(RIM + rows_n, RIM), :], halo_send.at[1], halo_recv.at[1], lax.rem(t + tiles - 1, tiles), d)
-
-    @pl.when(t > 0)
-    def _():
-        down.start()
 
     for k in range(1, NX):
         @pl.when(x_first[k])
@@ -216,20 +227,21 @@
             pl.semaphore_wait(z_ready.at[k - 1], 1)
             z_copies[k].start()
 
-    def arrive(k):
+    def arrival(k):
         block = gath.at[z_at(k), x]
-        remote(block, block, z_send.at[k - 1], z_recv.at[k - 1], t, date_at(z_at(k), x)).wait_recv()
-        spread(k, z_at(k))
-
-    def pass_on(of, to):
+        remote(block, block, z_send.at[0], z_recv.at[k - 1], t, date_at(z_at(k), x)).wait_recv()
+
+    near = jnp.where(zh == 0, 1, 3)
+    far = nz - near
+
+    def pass_on(of, to, sem):
         block = gath.at[z_at(of), x]
-        return remote(block, block, z_send.at[1], z_recv.at[1], t, date_at(z_at(to), x))
-
-    for k in range(1, NX):
-        @pl.when(jnp.logical_not(x_first[k]))
-        def _(k=k):
-            pl.semaphore_wait(x_ready.at[k - 1], 1)
-    spread_back(0, zh)
+        return remote(block, block, z_send.at[sem], z_recv.at[1], t, date_at(z_at(to), x))
+
+    passes = (
+        (zh <= 1, pass_on(near, far, 1)),
+        (zh == 0, pass_on(far, near, 3)),
+    )
 
     round_signal(0)
 
@@ -249,6 +261,10 @@
     weight = jnp.sum(jnp.where(picked, marks, 0.0), axis=1, keepdims=True)
     count = jnp.sum(marks, axis=1, keepdims=True) * float(cols_n)
 
+    round_wait(0)
+    round_signal(1)
+    turn(1)
+    turn(3)
     own_copy.wait()
 
     @pl.when(t > 0)
@@ -264,53 +280,74 @@
             part = jnp.dot(az_taps, ext[plane, :, pl.ds(b * BLOCK, BLOCK)], preferred_element_type=F32)
             azim[pl.ds(plane * rows_n, rows_n), pl.ds(SIDE + b * BLOCK, BLOCK)] = part.astype(BF16)
 
-    round_wait(0)
-    round_signal(1)
+
+    for k in range(1, NX):
+        @pl.when(jnp.logical_not(x_first[k]))
+        def _(k=k):
+            pl.semaphore_wait(x_ready.at[k - 1], 1)
+    spread_back(0, zh)
+
+    def take_near():
+        arrival(near)
+
+        @pl.when(passes[0][0])
+        def _():
+            passes[0][1].start()
+
+        spread(near, z_at(near))
+
+    @pl.when(zh != 2)
+    def _():
+        take_near()
+
+    round_wait(1)
+    round_signal(2)
+    def row_copy(plane, b):
+        piece = pl.ds(b * (BLOCK // 128), BLOCK // 128)
+        return remote(
+            res.at[piece, pl.ds(plane * rows_n, LAG), :], rnext.at[plane, piece], row_send.at[plane, b], row_recv.at[plane, b],
+            lax.rem(t + tiles - 1, tiles), d,
+        )
+
+    def send_rows(b):
+        @pl.when(t > 0)
+        def _():
+            row_copy(0, b).start()
+            row_copy(1, b).start()
 
     for b in range(cols_n // BLOCK):
         part = jnp.dot(azim[:, pl.ds(b * BLOCK, BLOCK + 2 * SIDE)], rg_taps, preferred_element_type=F32).astype(BF16)
         for h in range(BLOCK // 128):
             half = part[:, h * 128 : (h + 1) * 128]
             res[b * (BLOCK // 128) + h] = half
-
-    def row_copy(plane):
-        return remote(
-            res.at[:, pl.ds(plane * rows_n, LAG), :], rnext.at[plane], row_send.at[plane], row_recv.at[plane],
-            lax.rem(t + tiles - 1, tiles), d,
-        )
-
-    round_wait(1)
-    round_signal(2)
-
-    @pl.when(t > 0)
-    def _():
-        row_copy(0).start()
-        row_copy(1).start()
-
-    turn(1)
-    turn(3)
-    arrive(1)
-
-    @pl.when(zh == 0)
-    def _():
-        pass_on(1, 3).start()
+        if b > 0:
+            send_rows(b - 1)
+    send_rows(cols_n // BLOCK - 1)
+
 
     round_wait(2)
     round_signal(3)
-    arrive(3)
-
-    @pl.when(zh == 1)
-    def _():
-        pass_on(3, 1).start()
+    @pl.when(zh == 2)
+    def _():
+        take_near()
 
     round_wait(3)
     round_signal(4)
-    arrive(2)
+    arrival(far)
+
+    @pl.when(passes[1][0])
+    def _():
+        passes[1][1].start()
+
+    spread(far, z_at(far))
+    arrival(2)
+    spread(2, z_at(2))
 
     @pl.when(t < tiles - 1)
     def _():
-        row_copy(0).wait_recv()
-        row_copy(1).wait_recv()
+        for b in range(cols_n // BLOCK):
+            for plane in range(2):
+                row_copy(plane, b).wait_recv()
 
     low_half = iota((rows_n, 128), 1) < width
 
@@ -391,8 +428,17 @@
     out[0, 0] = looks_re * u_re + looks_im * u_im
     out[0, 1] = looks_im * u_re - looks_re * u_im
 
-    for k in range(1, nz):
-        z_copies[k].wait_send()
+    for copy in z_copies.values():
+        copy.wait_send()
+
+    @pl.when(zh == 2)
+    def _():
+        direct.wait_send()
+
+    for here, copy in passes:
+        @pl.when(here)
+        def _(copy=copy):
+            copy.wait_send()
     for group in range(nz):
         for k in range(1, NX):
             x_copy(group, z_at(group), k).wait_send()
@@ -407,8 +453,9 @@
         for group in range(nz):
             for k in range(NX):
                 next_copy(group, z_at(group), k).wait_send()
-        row_copy(0).wait_send()
-        row_copy(1).wait_send()
+        for b in range(cols_n // BLOCK):
+            for plane in range(2):
+                row_copy(plane, b).wait_send()
 
     pltpu.make_async_copy(stat_in, stat_in, stat_send).wait()
 
@@ -445,8 +492,8 @@
                 pltpu.VMEM((1, 1, 128), F32),
                 pltpu.VMEM((tiles - 1, 1, 128), F32),
                 pltpu.VMEM((2 * rows_n, 128), F32),
-                dma((7,)), dma((2,)), dma((2,)), dma((3,)), dma((3,)),
-                dma((nz, NX - 1)), dma((nz, NX - 1)), dma((nz, NX)), dma((nz, NX)), dma((2,)), dma((2,)), dma, dma,
+                dma((7,)), dma((2,)), dma((2,)), dma((4,)), dma((3,)),
+                dma((nz, NX - 1)), dma((nz, NX - 1)), dma((nz, NX)), dma((nz, NX)), dma((2, cols_n // BLOCK)), dma((2, cols_n // BLOCK)), dma, dma,
                 regular((nz - 1,)), regular((NX - 1,)), regular, regular((len(ROUNDS),)),
             ],
             compiler_params=pltpu.CompilerParams(collective_id=0, has_side_effects=True),

time: 37.2 us -> 36.2 us (0.973)
  Pallas kernels: 33.8 us -> 32.8 us
    pallas_call x1, Pallas kernels: 33.8 us -> 32.8 us  [shards(): pl.pallas_call(functools.partial(kernel, tiles, dates), out_shape=pltpu.V...]
where the time goes in v6:
time: 36.2 us; the launch traced here: 36 us
  Pallas kernels  32.8 us (91%)
  between operations  2.59 us (7%)
  local copies, waits for them, and re-layouts  0.62 us (2%)
    pallas_call x1, Pallas kernels, shards(): pl.pallas_call(functools.partial(kernel, tiles, dates), out_shape=pltpu.V...  32.8 us

profile of v6, /device:TPU:1, one launch (start us, length us, event | category | flops | bytes accessed | tf_op | source)
XLA Modules:
  0.0 36.0 jit_solution(4977828498125675054)
XLA Ops:
  2.6 32.8 %coregister.1 = f32[1,2,48,128]{3,2,1,0:T(8,128)S(1)} custom-call(bf16[1,2,96,1024]{3,2,1,0:T(8,128)(2,1)} %sec.1, bf16[128,96]{1,0:T(8,128)(2,1)} %bitcast.4, s32[1,96]{1,0:T(1,128)} %bitcast.5, s32[1,1]{1,0:T(1,128)S(6)} %copy.10.az_off_at, s32[1,1]{1,0:T(1,128)S(6)} %copy.11.rg_off_at, f32[1,1]{1,0:T(1,128)S(6)} %copy.12.az_frac_at, ...), custom_call_target="tpu_custom_call" | custom-call | tf_op jit(solution)/shard_map/coregister/pallas_call | solution.py:475
  35.4 0.6 %copy.9 = f32[1,2,48,128]{3,2,1,0:T(8,128)} copy(f32[1,2,48,128]{3,2,1,0:T(8,128)S(1)} %coregister.1) | data formatting | bytes 98304

commit v7 on v6

--- a/solution.py
+++ b/solution.py
@@ -48,6 +48,8 @@
     next_send, next_recv, row_send, row_recv, stat_send, stat_recv,
     z_ready, x_ready, tile_ready, round_ready,
 ):
+    prim_copy = pltpu.make_async_copy(prim, prim_in, local_sem.at[0])
+    prim_copy.start()
     nz = dates // NX
     rows_n = sec.shape[2]
     cols_n = sec.shape[3]
@@ -106,20 +108,8 @@
     ]
     for copy in small_copies:
         copy.start()
-    prim_copy = pltpu.make_async_copy(prim, prim_in, local_sem.at[0])
-    prim_copy.start()
     own_copy = pltpu.make_async_copy(sec.at[0], ext.at[:, pl.ds(RIM, rows_n), :], local_sem.at[1])
     own_copy.start()
-
-    @pl.when(t == 0)
-    def _():
-        ext[:, pl.ds(0, RIM), :] = jnp.zeros((2, RIM, cols_n), BF16)
-
-    @pl.when(t == tiles - 1)
-    def _():
-        ext[:, pl.ds(RIM + rows_n, RIM), :] = jnp.zeros((2, RIM, cols_n), BF16)
-        gnext[...] = jnp.zeros(gnext.shape, BF16)
-        rnext[...] = jnp.zeros(rnext.shape, BF16)
 
     mine = gath.at[zh, x]
 
@@ -141,13 +131,6 @@
     @pl.when(t > 0)
     def _():
         signal(tile_ready, t - 1, d)
-
-    up = remote(sec.at[0, :, pl.ds(rows_n - RIM, RIM), :], ext.at[:, pl.ds(0, RIM), :], halo_send.at[0], halo_recv.at[0], lax.rem(t + 1, tiles), d)
-    down = remote(sec.at[0, :, pl.ds(0, RIM), :], ext.at[:, pl.ds(RIM + rows_n, RIM), :], halo_send.at[1], halo_recv.at[1], lax.rem(t + tiles - 1, tiles), d)
-
-    @pl.when(t > 0)
-    def _():
-        down.start()
 
     prim_copy.wait()
     mine[...] = prim_in[...].astype(F32).T.astype(BF16)
@@ -168,7 +151,7 @@
         direct.start()
 
     for k in (1, nz - 1):
-        @pl.when(jnp.logical_not(z_first[k]))
+        @pl.when(jnp.logical_not(z_first[k]) & (zh != 2))
         def _(k=k):
             z_copies[k].start()
     for k in (2, 1, 3):
@@ -176,6 +159,13 @@
         def _(k=k):
             x_copy(0, zh, k).start()
 
+    up = remote(sec.at[0, :, pl.ds(rows_n - RIM, RIM), :], ext.at[:, pl.ds(0, RIM), :], halo_send.at[0], halo_recv.at[0], lax.rem(t + 1, tiles), d)
+    down = remote(sec.at[0, :, pl.ds(0, RIM), :], ext.at[:, pl.ds(RIM + rows_n, RIM), :], halo_send.at[1], halo_recv.at[1], lax.rem(t + tiles - 1, tiles), d)
+
+    @pl.when(t > 0)
+    def _():
+        down.start()
+
     for k in range(1, NX):
         @pl.when(x_first[k])
         def _(k=k):
@@ -187,6 +177,11 @@
     def _():
         pl.semaphore_wait(tile_ready, 1)
         up.start()
+
+    @pl.when(zh == 2)
+    def _():
+        z_copies[1].start()
+        z_copies[3].start()
 
     def round_signal(i):
         @pl.when(t >= ROUNDS[i])
@@ -244,6 +239,16 @@
     )
 
     round_signal(0)
+
+    @pl.when(t == 0)
+    def _():
+        ext[:, pl.ds(0, RIM), :] = jnp.zeros((2, RIM, cols_n), BF16)
+
+    @pl.when(t == tiles - 1)
+    def _():
+        ext[:, pl.ds(RIM + rows_n, RIM), :] = jnp.zeros((2, RIM, cols_n), BF16)
+        gnext[...] = jnp.zeros(gnext.shape, BF16)
+        rnext[...] = jnp.zeros(rnext.shape, BF16)
 
     for copy in small_copies:
         copy.wait()
@@ -398,11 +403,16 @@
         own = jnp.where(lane == k, jnp.sum(jnp.sum(v, axis=0, keepdims=True), axis=1, keepdims=True), own)
     stat_out[0] = own
 
-    def stat_copy(k):
-        return remote(stat_out, stat_in.at[pl.ds(tiles - 1 - k, 1)], stat_send, stat_recv, lax.rem(t + k, tiles), d)
-
-    for k in range(1, tiles):
-        stat_copy(k).start()
+    zl, y, core = t // 8, lax.rem(t // 2, 4), lax.rem(t, 2)
+    offsets = [(dz, dy, dc) for dy in (2, 1, 3, 0) for dz in (3, 1, 2, 0) for dc in (1, 0)][: tiles - 1]
+
+    def stat_copy(i):
+        dz, dy, dc = offsets[i]
+        tile = lax.rem(zl + dz, 4) * 8 + lax.rem(y + dy, 4) * 2 + lax.rem(core + dc, 2)
+        return remote(stat_out, stat_in.at[pl.ds(i, 1)], stat_send, stat_recv, tile, d)
+
+    for i in range(tiles - 1):
+        stat_copy(i).start()
 
     total = jnp.zeros((2 * rows_n, 128), F32)
     per = 128 // LR

time: 36.2 us -> 35.9 us (level)
  no operation moved by 1% of the time
where the time goes in v7:
time: 35.9 us; the launch traced here: 35.8 us
  Pallas kernels  32.6 us (91%)
  between operations  2.59 us (7%)
  local copies, waits for them, and re-layouts  0.62 us (2%)
    pallas_call x1, Pallas kernels, shards(): pl.pallas_call(functools.partial(kernel, tiles, dates), out_shape=pltpu.V...  32.6 us

profile of v7, /device:TPU:1, one launch (start us, length us, event | category | flops | bytes accessed | tf_op | source)
XLA Modules:
  0.0 35.8 jit_solution(9543131183401808375)
XLA Ops:
  2.6 32.6 %coregister.1 = f32[1,2,48,128]{3,2,1,0:T(8,128)S(1)} custom-call(bf16[1,2,96,1024]{3,2,1,0:T(8,128)(2,1)} %sec.1, bf16[128,96]{1,0:T(8,128)(2,1)} %bitcast.4, s32[1,96]{1,0:T(1,128)} %bitcast.5, s32[1,1]{1,0:T(1,128)S(6)} %copy.10.az_off_at, s32[1,1]{1,0:T(1,128)S(6)} %copy.11.rg_off_at, f32[1,1]{1,0:T(1,128)S(6)} %copy.12.az_frac_at, ...), custom_call_target="tpu_custom_call" | custom-call | tf_op jit(solution)/shard_map/coregister/pallas_call | solution.py:485
  35.2 0.6 %copy.9 = f32[1,2,48,128]{3,2,1,0:T(8,128)} copy(f32[1,2,48,128]{3,2,1,0:T(8,128)S(1)} %coregister.1) | data formatting | bytes 98304

commit v8 on v7

--- a/solution.py
+++ b/solution.py
@@ -270,6 +270,25 @@
     round_signal(1)
     turn(1)
     turn(3)
+    for k in range(1, NX):
+        @pl.when(jnp.logical_not(x_first[k]))
+        def _(k=k):
+            pl.semaphore_wait(x_ready.at[k - 1], 1)
+    spread_back(0, zh)
+
+    def take_near():
+        arrival(near)
+
+        @pl.when(passes[0][0])
+        def _():
+            passes[0][1].start()
+
+        spread(near, z_at(near))
+
+    @pl.when(zh != 2)
+    def _():
+        take_near()
+
     own_copy.wait()
 
     @pl.when(t > 0)
@@ -285,25 +304,6 @@
             part = jnp.dot(az_taps, ext[plane, :, pl.ds(b * BLOCK, BLOCK)], preferred_element_type=F32)
             azim[pl.ds(plane * rows_n, rows_n), pl.ds(SIDE + b * BLOCK, BLOCK)] = part.astype(BF16)
 
-
-    for k in range(1, NX):
-        @pl.when(jnp.logical_not(x_first[k]))
-        def _(k=k):
-            pl.semaphore_wait(x_ready.at[k - 1], 1)
-    spread_back(0, zh)
-
-    def take_near():
-        arrival(near)
-
-        @pl.when(passes[0][0])
-        def _():
-            passes[0][1].start()
-
-        spread(near, z_at(near))
-
-    @pl.when(zh != 2)
-    def _():
-        take_near()
 
     round_wait(1)
     round_signal(2)

time: 35.9 us -> 35.9 us (level)
  no operation moved by 1% of the time
where the time goes in v8:
time: 35.9 us; the launch traced here: 35.7 us
  Pallas kernels  32.5 us (91%)
  between operations  2.59 us (7%)
  local copies, waits for them, and re-layouts  0.62 us (2%)
    pallas_call x1, Pallas kernels, shards(): pl.pallas_call(functools.partial(kernel, tiles, dates), out_shape=pltpu.V...  32.5 us

profile of v8, /device:TPU:1, one launch (start us, length us, event | category | flops | bytes accessed | tf_op | source)
XLA Modules:
  0.0 35.7 jit_solution(5062476712161628360)
XLA Ops:
  2.6 32.5 %coregister.1 = f32[1,2,48,128]{3,2,1,0:T(8,128)S(1)} custom-call(bf16[1,2,96,1024]{3,2,1,0:T(8,128)(2,1)} %sec.1, bf16[128,96]{1,0:T(8,128)(2,1)} %bitcast.4, s32[1,96]{1,0:T(1,128)} %bitcast.5, s32[1,1]{1,0:T(1,128)S(6)} %copy.10.az_off_at, s32[1,1]{1,0:T(1,128)S(6)} %copy.11.rg_off_at, f32[1,1]{1,0:T(1,128)S(6)} %copy.12.az_frac_at, ...), custom_call_target="tpu_custom_call" | custom-call | tf_op jit(solution)/shard_map/coregister/pallas_call | solution.py:485
  35.1 0.6 %copy.9 = f32[1,2,48,128]{3,2,1,0:T(8,128)} copy(f32[1,2,48,128]{3,2,1,0:T(8,128)S(1)} %coregister.1) | data formatting | bytes 98304
